TPU v7x, 32 devices: a whole 2x2x4 slice. The times are simulated.
32 devices in a mesh: user: 4 (over y, x), item: 8 (over z, core).
Axes of the slice: x: 2, y: 2, z: 4, core: 2. Of those that a mesh axis runs over, the one named last changes fastest.
Arguments:
- item_factors: bfloat16 [16384, 256], P('item'), may hold values from -0.125 to 0.125
- item_gram: float32 [256, 256], replicated, as said below
- tile_users: int32 [4, 8, 48], P('user', 'item'), may hold values from 0 to 3
- tile_items: int32 [4, 8, 48], P('user', 'item'), may hold values from 0 to 15, as said below
- tile_counts: int32 [4, 8], P('user', 'item'), may hold values from 12 to 48, as said below
- tile_values: bfloat16 [4, 8, 48, 128, 128], P('user', 'item'), may hold values from 0 to 8
Outputs:
- user_factors: float32 [2048, 256], P(('user', 'item'))
- item_rhs: float32 [8, 2048, 256], P('item', 'user')
Inputs may be any that keep to these rules, and one draw needn't show every extreme that they name: `item_gram`: symmetric positive definite. The pairs (tile_users, tile_items) of one device's slots are all different. `tile_counts`: some device uses all 48 slots in every draw.
All inputs are finite; a program needn't handle non-finite values.
Results may differ from a plain program's by a relative error of at most 0.0032.
Values may be sent and summed in bfloat16 or wider, within the bound.
A program may use at most 64 MiB of HBM per device.

v0:
```python
import jax
import jax.numpy as jnp
from jax import lax
from jax.sharding import PartitionSpec as P

USER_BLK = 4
ITERS = 3


epsilon = 1e-06
highest = lax.Precision.HIGHEST


def tile_runner(tile_work, arrays, tile_count):
    slots = arrays[0].shape[0]
    active = jnp.arange(slots, dtype=jnp.int32) < tile_count
    return tile_work(arrays, active)


def chosen_of(block_ids, active, limit):
    return (
        (block_ids[:, None] == jnp.arange(limit, dtype=jnp.int32)[None, :]) & active[:, None]
    ).astype(jnp.float32)


def reduce_rows(partial_value):
    return lax.psum_scatter(partial_value, "item", scatter_dimension=0, tiled=True)


def spread_rows(user_rows):
    return lax.all_gather(user_rows, "item", axis=0, tiled=True)


def local(item_factors, item_gram, tile_users, tile_items, tile_counts, tile_values):
    rank_width = item_factors.shape[1]
    tile_side = tile_values.shape[-1]
    block_grid_height = item_factors.reshape(-1, tile_side, rank_width)
    item_blocks = block_grid_height.shape[0]
    user_ids = tile_users[0, 0]
    item_ids = tile_items[0, 0]
    tile_vals = tile_values[0, 0]
    tile_count = tile_counts[0, 0]
    group_rows = USER_BLK * tile_side
    confidence = jnp.where(tile_vals > 0, 1.0 + tile_vals.astype(jnp.float32), 0.0).astype(
        jnp.bfloat16
    )

    def rhs_work(pieces, active):
        users_here, items_here, conf_here = pieces
        item_rows = jnp.take(block_grid_height, items_here, axis=0)
        partial_value = jnp.einsum(
            "tui,tir->tur", conf_here, item_rows, preferred_element_type=jnp.float32
        )
        return jnp.einsum(
            "tk,tur->kur", chosen_of(users_here, active, USER_BLK), partial_value, precision=highest
        )

    def make_apply(dir_rows):

        def apply_work(pieces, active):
            users_here, items_here, vals_here = pieces
            item_rows = jnp.take(block_grid_height, items_here, axis=0)
            user_rows = jnp.take(dir_rows, users_here, axis=0)
            scores = jnp.einsum(
                "tur,tir->tui", user_rows, item_rows, preferred_element_type=jnp.float32
            )
            weighted = (scores * vals_here.astype(jnp.float32)).astype(jnp.bfloat16)
            returned = jnp.einsum(
                "tui,tir->tur", weighted, item_rows, preferred_element_type=jnp.float32
            )
            return jnp.einsum(
                "tk,tur->kur", chosen_of(users_here, active, USER_BLK), returned, precision=highest
            )

        return apply_work

    rhs_part = tile_runner(rhs_work, (user_ids, item_ids, confidence), tile_count)
    right_side = reduce_rows(rhs_part.reshape(group_rows, rank_width))
    solution = jnp.zeros_like(right_side)
    residual = right_side
    direction = right_side
    norm_now = jnp.sum(residual * residual, axis=1, keepdims=True)
    for iteration in range(ITERS):
        dir_rows = spread_rows(direction.astype(jnp.bfloat16)).reshape(
            USER_BLK, tile_side, rank_width
        )
        tile_part = tile_runner(make_apply(dir_rows), (user_ids, item_ids, tile_vals), tile_count)
        image = jnp.dot(direction, item_gram, precision=highest) + reduce_rows(
            tile_part.reshape(group_rows, rank_width)
        )
        step_size = norm_now / (jnp.sum(direction * image, axis=1, keepdims=True) + epsilon)
        solution = solution + step_size * direction
        residual = residual - step_size * image
        norm_next = jnp.sum(residual * residual, axis=1, keepdims=True)
        direction = residual + norm_next / (norm_now + epsilon) * direction
        norm_now = norm_next
    closing_rows = spread_rows(solution.astype(jnp.bfloat16)).reshape(
        USER_BLK, tile_side, rank_width
    )

    def item_work(pieces, active):
        users_here, items_here, conf_here = pieces
        user_rows = jnp.take(closing_rows, users_here, axis=0)
        partial_value = jnp.einsum(
            "tui,tur->tir", conf_here, user_rows, preferred_element_type=jnp.float32
        )
        return jnp.einsum(
            "tk,tir->kir",
            chosen_of(items_here, active, item_blocks),
            partial_value,
            precision=highest,
        )

    item_part = tile_runner(item_work, (user_ids, item_ids, confidence), tile_count)
    item_part = item_part.reshape(1, item_blocks * tile_side, rank_width)
    users_total = lax.axis_size("user") * group_rows
    item_rhs = lax.psum_scatter(
        item_part, "user", scatter_dimension=1, tiled=True
    ) * users_total ** (-0.5)
    return (solution, item_rhs)


def solution(mesh):
    return jax.shard_map(
        local,
        mesh=mesh,
        in_specs=(
            P("item", None),
            P(),
            P("user", "item", None),
            P("user", "item", None),
            P("user", "item"),
            P("user", "item", None, None, None),
        ),
        out_specs=(P(("user", "item"), None), P("item", "user", None)),
        check_vma=False,
    )
```

profile of v0, /device:TPU:0, one launch (start us, length us, event | category | flops | bytes accessed | tf_op | source)
XLA Modules:
  0.0 324.9 jit_solution(11120795216845074523)
XLA Ops:
  7.2 0.0 copy-start
  7.2 0.0 reduce-scatter.6.cloned.1.call-start
  7.2 0.7 compare_and_fusion.1
  8.0 0.7 compare_select_fusion.1
  9.3 0.7 fusion.68
  10.0 0.0 copy-done
  10.0 0.0 copy-start.1
  10.0 2.6 gather_fusion
  12.5 0.0 copy-done.1
  12.5 2.9 fusion.58
  15.5 0.0 copy-start.5
  15.5 5.7 %fusion.8 = f32[4,128,256]{2,0,1:T(4,128)S(1)} fusion(pred[48,4,1]{0,1,2:T(4,128)(4,1)S(1)} %fusion.68, f32[48,128,256]{2,1,0:T(8,128)S(1)} %fusion.58), kind=kOutput, calls=%fused_computation.13 | convolution fusion | flops 75497472 | bytes 6815936 | tf_op jit(solution)/shard_map/tk,tur->kur/dot_general | solution.py:54
  21.1 0.9 copy.11
  22.0 0.0 reduce-scatter.6.cloned.1.call-update
  22.1 0.0 reduce-scatter.8.cloned.1.call-start
  22.1 0.0 copy-done.5
  22.2 33.9 %reduce-scatter.6.cloned.1.call-done = f32[64,256]{1,0:T(8,128)} async-done(((f32[512,256]{1,0:T(8,128)}), f32[64,256]{1,0:T(8,128)}) %reduce-scatter.6.cloned.1.call-update) | async-done | bytes 65552 | tf_op jit(solution)/shard_map/reduce_scatter | solution.py:27
  56.1 0.8 convert_element_type.41
  56.9 14.7 %all_gather.12 = bf16[512,256]{1,0:T(8,128)(2,1)S(1)} all-gather(bf16[64,256]{1,0:T(8,128)(2,1)S(1)} %convert_element_type.41), channel_id=1, replica_groups=mesh['user'=4,'item'=8] {'item'}, dimensions={0}, use_global_device_ids=true | all-gather | bytes 294912 | tf_op jit(solution)/shard_map/all_gather | solution.py:31
  71.6 2.5 gather_fusion.1
  74.1 8.4 %fusion.39 = f32[48,128,256]{2,1,0:T(8,128)} fusion(bf16[48,128,256]{2,1,0:T(8,128)(2,1)} %gather_fusion.1, pred[48]{0:T(512)(128)(4,1)S(1)} %compare_and_fusion, bf16[1,1,48,128,128]{4,3,2,1,0:T(8,128)(2,1)S(1)} %copy-done.1, bf16[48,128,256]{2,1,0:T(8,128)(2,1)} %gather_fusion, pred[48]{0:T(512)(128)(4,1)S(1)} %compare_and_fusion.1), kind=kOutput, calls=%fused_computation.39 | convolution fusion | flops 812384256 | bytes 14155872 | tf_op jit(solution)/shard_map/tui,tir->tur/dot_general | solution.py:68
  82.5 0.0 copy-start.2
  82.5 0.0 copy-start.3
  82.5 8.1 %fusion.6 = f32[4,128,256]{2,0,1:T(4,128)S(1)} fusion(pred[48,4,1]{0,1,2:T(4,128)(4,1)S(1)} %fusion.68, f32[48,128,256]{2,1,0:T(8,128)} %fusion.39), kind=kOutput, calls=%fused_computation.11 | convolution fusion | flops 75497472 | bytes 6815936 | tf_op jit(solution)/shard_map/tk,tur->kur/dot_general | solution.py:71
  90.6 0.9 copy.12
  91.5 0.0 reduce-scatter.8.cloned.1.call-update
  91.5 0.0 reduce-scatter.10.cloned.1.call-start
  91.6 29.8 %reduce-scatter.8.cloned.1.call-done = f32[64,256]{1,0:T(8,128)} async-done(((f32[512,256]{1,0:T(8,128)}), f32[64,256]{1,0:T(8,128)}) %reduce-scatter.8.cloned.1.call-update) | async-done | bytes 65552 | tf_op jit(solution)/shard_map/reduce_scatter | solution.py:27
  121.3 0.0 copy-done.2
  121.3 0.0 copy-done.3
  121.3 1.2 multiply_reduce_fusion.3
  122.6 0.2 multiply_reduce_fusion.2
  122.8 0.1 fusion.84
  122.9 14.4 %all_gather.13 = bf16[512,256]{1,0:T(8,128)(2,1)S(1)} all-gather(bf16[64,256]{1,0:T(8,128)(2,1)S(1)} %get-tuple-element.10), channel_id=1, replica_groups=mesh['user'=4,'item'=8] {'item'}, dimensions={0}, use_global_device_ids=true | all-gather | bytes 294912 | tf_op jit(solution)/shard_map/all_gather | solution.py:31
  137.2 2.5 gather_fusion.2
  139.7 8.4 %fusion.33 = f32[48,128,256]{2,1,0:T(8,128)} fusion(bf16[48,128,256]{2,1,0:T(8,128)(2,1)} %gather_fusion.2, pred[48]{0:T(512)(128)(4,1)S(1)} %compare_and_fusion, bf16[1,1,48,128,128]{4,3,2,1,0:T(8,128)(2,1)S(1)} %copy-done.1, bf16[48,128,256]{2,1,0:T(8,128)(2,1)} %gather_fusion, pred[48]{0:T(512)(128)(4,1)S(1)} %compare_and_fusion.1), kind=kOutput, calls=%fused_computation.38 | convolution fusion | flops 812384256 | bytes 14155872 | tf_op jit(solution)/shard_map/tui,tir->tur/dot_general | solution.py:68
  148.1 8.1 %fusion.4 = f32[4,128,256]{2,0,1:T(4,128)S(1)} fusion(pred[48,4,1]{0,1,2:T(4,128)(4,1)S(1)} %fusion.68, f32[48,128,256]{2,1,0:T(8,128)} %fusion.33), kind=kOutput, calls=%fused_computation.9 | convolution fusion | flops 75497472 | bytes 6815936 | tf_op jit(solution)/shard_map/tk,tur->kur/dot_general | solution.py:71
  156.2 0.9 copy.13
  157.0 0.0 reduce-scatter.10.cloned.1.call-update
  157.1 0.0 reduce-scatter.12.cloned.1.call-start
  157.1 29.6 %reduce-scatter.10.cloned.1.call-done = f32[64,256]{1,0:T(8,128)} async-done(((f32[512,256]{1,0:T(8,128)}), f32[64,256]{1,0:T(8,128)}) %reduce-scatter.10.cloned.1.call-update) | async-done | bytes 65552 | tf_op jit(solution)/shard_map/reduce_scatter | solution.py:27
  186.8 1.2 multiply_reduce_fusion.1
  188.0 0.2 multiply_reduce_fusion
  188.2 0.1 fusion.83
  188.3 14.4 %all_gather.14 = bf16[512,256]{1,0:T(8,128)(2,1)S(1)} all-gather(bf16[64,256]{1,0:T(8,128)(2,1)S(1)} %get-tuple-element.8), channel_id=1, replica_groups=mesh['user'=4,'item'=8] {'item'}, dimensions={0}, use_global_device_ids=true | all-gather | bytes 294912 | tf_op jit(solution)/shard_map/all_gather | solution.py:31
  202.7 2.5 gather_fusion.3
  205.2 8.3 %fusion.27 = f32[48,128,256]{2,1,0:T(8,128)} fusion(bf16[48,128,256]{2,1,0:T(8,128)(2,1)} %gather_fusion.3, pred[48]{0:T(512)(128)(4,1)S(1)} %compare_and_fusion, bf16[1,1,48,128,128]{4,3,2,1,0:T(8,128)(2,1)S(1)} %copy-done.1, bf16[48,128,256]{2,1,0:T(8,128)(2,1)} %gather_fusion, pred[48]{0:T(512)(128)(4,1)S(1)} %compare_and_fusion.1), kind=kOutput, calls=%fused_computation.37 | convolution fusion | flops 812384256 | bytes 14155872 | tf_op jit(solution)/shard_map/tui,tir->tur/dot_general | solution.py:68
  213.5 8.1 %fusion.2 = f32[4,128,256]{2,0,1:T(4,128)S(1)} fusion(pred[48,4,1]{0,1,2:T(4,128)(4,1)S(1)} %fusion.68, f32[48,128,256]{2,1,0:T(8,128)} %fusion.27), kind=kOutput, calls=%fused_computation.7 | convolution fusion | flops 75497472 | bytes 6815936 | tf_op jit(solution)/shard_map/tk,tur->kur/dot_general | solution.py:71
  221.6 0.9 copy.14
  222.5 0.0 reduce-scatter.12.cloned.1.call-update
  222.5 0.0 reduce-scatter.14.cloned.1.call-start
  222.6 29.8 %reduce-scatter.12.cloned.1.call-done = f32[64,256]{1,0:T(8,128)} async-done(((f32[512,256]{1,0:T(8,128)}), f32[64,256]{1,0:T(8,128)}) %reduce-scatter.12.cloned.1.call-update) | async-done | bytes 65552 | tf_op jit(solution)/shard_map/reduce_scatter | solution.py:27
  252.4 1.2 fusion.56
  253.6 0.7 fusion.82
  254.3 14.4 %all_gather.15 = bf16[512,256]{1,0:T(8,128)(2,1)S(1)} all-gather(bf16[64,256]{1,0:T(8,128)(2,1)S(1)} %get-tuple-element.6), channel_id=1, replica_groups=mesh['user'=4,'item'=8] {'item'}, dimensions={0}, use_global_device_ids=true | all-gather | bytes 294912 | tf_op jit(solution)/shard_map/all_gather | solution.py:31
  268.8 2.5 gather_fusion.4
  271.3 0.0 copy-start.4
  271.3 3.0 fusion.15
  274.3 0.0 copy-done.4
  274.3 5.8 %fusion = f32[16,128,256]{2,0,1:T(8,128)S(1)} fusion(f32[48,128,256]{2,1,0:T(8,128)S(1)} %fusion.15, s32[48]{0:T(128)S(1)} %bitcast.66, pred[48]{0:T(512)(128)(4,1)S(1)} %iota_compare_fusion.2), kind=kOutput, calls=%fused_computation.5 | convolution fusion | flops 301991424 | bytes 8388848 | tf_op jit(solution)/shard_map/tk,tir->kir/dot_general | solution.py:107
  280.1 2.6 copy.15
  282.7 0.0 reduce-scatter.14.cloned.1.call-update
  282.7 33.5 %reduce-scatter.14.cloned.1.call-done = f32[1,512,256]{2,1,0:T(8,128)} async-done(((f32[1,2048,256]{2,1,0:T(8,128)}), f32[1,512,256]{2,1,0:T(8,128)}) %reduce-scatter.14.cloned.1.call-update) | async-done | bytes 524304 | tf_op jit(solution)/shard_map/reduce_scatter | solution.py:117
  316.2 1.9 broadcast_multiply_fusion
  (10 shorter events, 0.1 us)
Async XLA Ops:
  7.2 2.8 copy-start
  7.2 48.9 %reduce-scatter.6.cloned.1.call-start = ((), (), s32[]{:S(2)}) async-start(), calls=%async_computation.5 | async-start | bytes 589824 | tf_op jit(solution)/shard_map/reduce_scatter | solution.py:27
  10.0 2.6 copy-start.1
  15.5 6.6 %copy-start.5 = (s32[1,1,48]{2,1,0:T(1,128)S(1)}, s32[1,1,48]{2,1,0:T(1,128)}, u32[]{:S(2)}) copy-start(s32[1,1,48]{2,1,0:T(1,128)} %param.12) | copy-start | bytes 580
  22.1 99.3 %reduce-scatter.8.cloned.1.call-start = ((), (), s32[]{:S(2)}) async-start(), calls=%async_computation.6 | async-start | bytes 589824 | tf_op jit(solution)/shard_map/reduce_scatter | solution.py:27
  82.5 38.9 %copy-start.2 = (f32[256,256]{1,0:T(8,128)S(1)}, f32[256,256]{1,0:T(8,128)}, u32[]{:S(2)}) copy-start(f32[256,256]{1,0:T(8,128)} %param.11) | copy-start | bytes 786436
  82.5 38.9 %copy-start.3 = (f32[64,256]{1,0:T(8,128)S(1)}, f32[64,256]{1,0:T(8,128)}, u32[]{:S(2)}) copy-start(f32[64,256]{1,0:T(8,128)} %reduce-scatter.6.cloned.1.call-done) | copy-start | bytes 196612
  91.5 95.2 %reduce-scatter.10.cloned.1.call-start = ((), (), s32[]{:S(2)}) async-start(), calls=%async_computation.7 | async-start | bytes 589824 | tf_op jit(solution)/shard_map/reduce_scatter | solution.py:27
  157.1 95.3 %reduce-scatter.12.cloned.1.call-start = ((), (), s32[]{:S(2)}) async-start(), calls=%async_computation.8 | async-start | bytes 589824 | tf_op jit(solution)/shard_map/reduce_scatter | solution.py:27
  222.5 93.7 %reduce-scatter.14.cloned.1.call-start = ((), (), s32[]{:S(2)}) async-start(), calls=%async_computation.9 | async-start | bytes 2621440 | tf_op jit(solution)/shard_map/reduce_scatter | solution.py:117
  271.3 3.0 copy-start.4
Sparse Core Ops, SparseCore 0:
  22.2 33.8 reduce-scatter.5
  91.7 29.6 reduce-scatter.7
  157.2 29.5 reduce-scatter.9
  222.6 29.7 reduce-scatter.11
  282.8 33.3 reduce-scatter.13
where the time goes:
time: 331 us; the launch traced here: 325 us
  waiting for transfers between devices  157 us (47%)
  matrix products  70.4 us (21%)
  blocking collectives  57.9 us (17%)
  local copies, waits for them, and re-layouts  18.7 us (6%)
  between operations  14.9 us (5%)
  other arithmetic  6.15 us (2%)
    reduce_scatter x4, waiting for transfers between devices, reduce_rows(): lax.psum_scatter(partial_value, 'item', scatter_dimension=0, tiled=True)  123 us
    all_gather x4, blocking collectives, spread_rows(): return lax.all_gather(user_rows, 'item', axis=0, tiled=True)  57.9 us
    reduce_scatter x1, waiting for transfers between devices, local(): lax.psum_scatter(item_part, 'user', scatter_dimension=1, tiled=True)  33.5 us
    dot_general x3, matrix products, apply_work(): jnp.einsum('tui,tir->tur', weighted, item_rows, preferred_element_type=jn...  25.1 us
    dot_general x3, matrix products, apply_work(): jnp.einsum('tk,tur->kur', chosen_of(users_here, active, USER_BLK), return...  24.4 us
    gather x3, local copies, waits for them, and re-layouts, apply_work(): user_rows = jnp.take(dir_rows, users_here, axis=0)  7.44 us
  transfers between devices with their start and end apart: 5, of which 5 were waited for; matrix products, arithmetic and copies ran while one was open for 0% of the time, Pallas kernels for 0%

commit v1 on v0

v1 whole, which is shorter than its diff:
```python
import functools

import jax
import jax.numpy as jnp
from jax import lax
from jax.experimental import pallas as pl
from jax.experimental.pallas import tpu as pltpu
from jax.sharding import PartitionSpec as P

USER_BLK = 4
ITERS = 3
CHUNK = 256

epsilon = 1e-06
highest = lax.Precision.HIGHEST
MESH = pl.DeviceIdType.MESH
NT = (((1,), (1,)), ((), ()))


def confidence_of(w):
    w = w.astype(jnp.float32)
    return jnp.where(w > 0, 1.0 + w, 0.0).astype(jnp.bfloat16)


def kernel(
    nu, ni, scale,
    inv_ref, y_hbm, gram_hbm, tiles_hbm,
    sol_ref, item_ref,
    tiles, yv, gram, wide, wx, ct, xall, dirs, part, ra, sb, rb,
    load_sem, w_send, w_recv, a_send, a_recv, b_send, b_recv,
    z_send, z_recv, f_send, f_recv, u_send, u_recv, s_send, s_recv,
):
    slots, side, _ = tiles_hbm.shape
    items, rank = yv.shape
    group = wide.shape[0]
    rows = group // ni
    nz = ni // 2
    cols = items // nu
    blocks = items // side
    g, o = lax.axis_index("user"), lax.axis_index("item")
    z, c = lax.div(o, 2), lax.rem(o, 2)
    other = 1 - c
    sib = {"item": z * 2 + other}

    def znum(j):
        return lax.rem(z + (j + nz), nz)

    def unum(j):
        return lax.rem(g + (j + nu), nu)

    def zpeer(j):
        return {"item": znum(j) * 2 + c}

    def upeer(j):
        return {"user": unum(j)}

    def row(zz, cc):
        return pl.ds(pl.multiple_of((zz * 2 + cc) * rows, rows), rows)

    def xrow(gg, zz, cc):
        return pl.ds(pl.multiple_of(gg * group + (zz * 2 + cc) * rows, rows), rows)

    def zrow(zz):
        return pl.ds(pl.multiple_of(zz * rows, rows), rows)

    sent = []

    def rcopy(src, dst, ss, rs, dev):
        return pltpu.make_async_remote_copy(
            src_ref=src, dst_ref=dst, send_sem=ss, recv_sem=rs, device_id=dev, device_id_type=MESH
        )

    def send(*args):
        cp = rcopy(*args)
        cp.start()
        sent.append(cp)

    def arrived(dst, ss, rs, dev):
        rcopy(dst, dst, ss, rs, dev).wait_recv()

    loads = [
        pltpu.make_async_copy(tiles_hbm, tiles.at[pl.ds(0, slots)], load_sem.at[0]),
        pltpu.make_async_copy(y_hbm, yv, load_sem.at[1]),
        pltpu.make_async_copy(gram_hbm, gram, load_sem.at[2]),
    ]
    for cp in loads:
        cp.start()

    barrier = pltpu.get_barrier_semaphore()
    pl.semaphore_signal(barrier, inc=1, device_id=sib, device_id_type=MESH)
    for j in range(1, nz):
        pl.semaphore_signal(barrier, inc=1, device_id=zpeer(j), device_id_type=MESH)
    for j in range(1, nu):
        pl.semaphore_signal(barrier, inc=1, device_id=upeer(j), device_id_type=MESH)

    tiles[slots] = jnp.zeros((side, side), jnp.bfloat16)
    loads[0].wait()
    for u in range(USER_BLK):
        for b in range(blocks):
            wide[u * side : (u + 1) * side, b * side : (b + 1) * side] = tiles[inv_ref[u * blocks + b]]
    for cp in loads[1:]:
        cp.wait()
    pl.semaphore_wait(barrier, nz + nu - 1)

    def wcol(gg):
        return pl.ds(pl.multiple_of(gg * cols, cols), cols)

    for j in range(1, nu):
        send(wide.at[:, wcol(unum(j))], wx.at[j], w_send.at[j], w_recv.at[j], upeer(j))

    def turn(j):
        if j == 0:
            block = wide[:, wcol(g)]
        else:
            arrived(wx.at[j], w_send.at[j], w_recv.at[j], upeer(-j))
            block = wx[j]
        ct[j] = confidence_of(block).T

    turns = [[], [], [], []]
    for j in range(nu):
        turns[j * 4 // nu].append(j)

    def step_of(i):
        return pl.ds(pl.multiple_of(i * CHUNK, CHUNK), CHUNK)

    def rhs_pass():
        part[0] = jnp.zeros((group, rank), jnp.float32)

        def body(i, _):
            at = step_of(i)
            part[0] += jnp.dot(confidence_of(wide[:, at]), yv[at, :], preferred_element_type=jnp.float32)
            return 0

        lax.fori_loop(0, items // CHUNK, body, 0)

    def apply_pass(k):
        part[k] = jnp.zeros((group, rank), jnp.float32)

        def body(i, _):
            at = step_of(i)
            yc = yv[at, :]
            scores = lax.dot_general(dirs[k - 1], yc, NT, preferred_element_type=jnp.float32)
            weighted = (scores * wide[:, at].astype(jnp.float32)).astype(jnp.bfloat16)
            part[k] += jnp.dot(weighted, yc, preferred_element_type=jnp.float32)
            return 0

        lax.fori_loop(0, items // CHUNK, body, 0)

    order = list(range(1, nz)) + [0]

    def reduce_start(k):
        for j in order:
            zz = znum(j)
            send(part.at[k, row(zz, other)], ra.at[k, zrow(zz)], a_send.at[k, j], a_recv.at[k, j], sib)
        own = None
        for j in order:
            zz = znum(j)
            arrived(ra.at[k, zrow(zz)], a_send.at[k, j], a_recv.at[k, j], sib)
            total = part[k, row(zz, c)] + ra[k, zrow(zz)]
            if j:
                sb[k, zrow(zz)] = total.astype(jnp.bfloat16)
                send(sb.at[k, zrow(zz)], rb.at[k, zrow(z)], b_send.at[k, j], b_recv.at[k, j], zpeer(j))
            else:
                own = total
        return own

    def reduce_end(k, own):
        for j in range(1, nz):
            src = zrow(znum(-j))
            arrived(rb.at[k, src], b_send.at[k, j], b_recv.at[k, j], zpeer(-j))
            own = own + rb[k, src].astype(jnp.float32)
        return own

    def gather(k, value, filler):
        buf = dirs.at[k]
        mine = row(z, c)
        buf[mine, :] = value.astype(jnp.bfloat16)
        for j in range(1, nz):
            send(buf.at[mine], buf.at[mine], z_send.at[k, j], z_recv.at[k, j], zpeer(j))
        send(buf.at[mine], buf.at[mine], f_send.at[k, 0], f_recv.at[k, 0], sib)
        filler()
        for j in range(1, nz):
            src = row(znum(-j), c)
            arrived(buf.at[src], z_send.at[k, j], z_recv.at[k, j], zpeer(-j))
            send(buf.at[src], buf.at[src], f_send.at[k, j], f_recv.at[k, j], sib)
        for j in range(nz):
            src = row(znum(-j), other)
            arrived(buf.at[src], f_send.at[k, j], f_recv.at[k, j], sib)

    def nothing():
        pass

    def turn_all(which):
        for j in turns[which]:
            turn(j)

    rhs_pass()
    own = reduce_start(0)
    residual = reduce_end(0, own)
    direction = residual
    sol = jnp.zeros_like(residual)
    norm = jnp.sum(residual * residual, axis=1, keepdims=True)
    for k in range(1, ITERS + 1):
        gather(k - 1, direction, functools.partial(turn_all, 2) if k == ITERS else nothing)
        apply_pass(k)
        own = reduce_start(k)
        image = jnp.dot(direction, gram[...], precision=highest, preferred_element_type=jnp.float32)
        if k == 1:
            turn_all(0)
        elif k == 2:
            turn_all(1)
        elif k == ITERS:
            turn_all(3)
        image = image + reduce_end(k, own)
        alpha = norm / (jnp.sum(direction * image, axis=1, keepdims=True) + epsilon)
        sol = sol + alpha * direction
        if k < ITERS:
            residual = residual - alpha * image
            norm_next = jnp.sum(residual * residual, axis=1, keepdims=True)
            direction = residual + norm_next / (norm + epsilon) * direction
            norm = norm_next

    mine = xrow(g, z, c)
    xall[mine, :] = sol.astype(jnp.bfloat16)
    k = ITERS

    def share(piece, j):
        for v in range(1, nu):
            send(xall.at[piece], xall.at[piece], u_send.at[v, j], u_recv.at[v, j], upeer(v))
        send(xall.at[piece], xall.at[piece], s_send.at[0, j], s_recv.at[0, j], sib)

    for j in range(1, nz):
        send(xall.at[mine], xall.at[mine], z_send.at[k, j], z_recv.at[k, j], zpeer(j))
    share(mine, 0)
    sol_ref[...] = sol
    for j in range(1, nz):
        piece = xrow(g, znum(-j), c)
        arrived(xall.at[piece], z_send.at[k, j], z_recv.at[k, j], zpeer(-j))
        share(piece, j)

    def finish(v):
        src = unum(-v)
        for j in range(nz):
            arrived(xall.at[xrow(src, znum(-j), other)], s_send.at[v, j], s_recv.at[v, j], sib)
        here = pl.ds(pl.multiple_of(src * group, group), group)
        return jnp.dot(ct[v], xall[here, :], preferred_element_type=jnp.float32)

    for v in range(1, nu):
        for j in range(nz):
            piece = xrow(unum(-v), znum(-j), c)
            arrived(xall.at[piece], u_send.at[v, j], u_recv.at[v, j], upeer(-v))
            send(xall.at[piece], xall.at[piece], s_send.at[v, j], s_recv.at[v, j], sib)
        if v == 1:
            item_ref[...] = finish(0)
        else:
            item_ref[...] += finish(v - 1)
    item_ref[...] = (item_ref[...] + finish(nu - 1)) * scale
    for cp in sent:
        cp.wait_send()


def make_local(nu, ni):
    def local(item_factors, item_gram, tile_users, tile_items, tile_counts, tile_values):
        items, rank = item_factors.shape
        slots, side = tile_values.shape[2], tile_values.shape[-1]
        blocks = items // side
        group = USER_BLK * side
        rows = group // ni
        nz = ni // 2
        cols = items // nu
        at = jnp.arange(slots, dtype=jnp.int32)
        key = jnp.where(at < tile_counts[0, 0], tile_users[0, 0] * blocks + tile_items[0, 0], -1)
        match = key[None, :] == jnp.arange(USER_BLK * blocks, dtype=jnp.int32)[:, None]
        inv = slots - jnp.sum(jnp.where(match, slots - at[None, :], 0), axis=1)
        scale = float(nu * group) ** -0.5
        bf, f4 = jnp.bfloat16, jnp.float32
        dma = pltpu.SemaphoreType.DMA
        rounds = ITERS + 1
        anywhere = pl.BlockSpec(memory_space=pl.ANY)
        vmem = pl.BlockSpec(memory_space=pltpu.VMEM)
        sol, item = pl.pallas_call(
            functools.partial(kernel, nu, ni, scale),
            out_shape=(
                jax.ShapeDtypeStruct((rows, rank), f4),
                jax.ShapeDtypeStruct((cols, rank), f4),
            ),
            in_specs=[pl.BlockSpec(memory_space=pltpu.SMEM), anywhere, anywhere, anywhere],
            out_specs=(vmem, vmem),
            scratch_shapes=[
                pltpu.VMEM((slots + 1, side, side), bf),
                pltpu.VMEM((items, rank), bf),
                pltpu.VMEM((rank, rank), f4),
                pltpu.VMEM((group, items), bf),
                pltpu.VMEM((nu, group, cols), bf),
                pltpu.VMEM((nu, cols, group), bf),
                pltpu.VMEM((nu * group, rank), bf),
                pltpu.VMEM((ITERS, group, rank), bf),
                pltpu.VMEM((rounds, group, rank), f4),
                pltpu.VMEM((rounds, nz * rows, rank), f4),
                pltpu.VMEM((rounds, nz * rows, rank), bf),
                pltpu.VMEM((rounds, nz * rows, rank), bf),
                dma((3,)),
                dma((nu,)), dma((nu,)),
                dma((rounds, nz)), dma((rounds, nz)),
                dma((rounds, nz)), dma((rounds, nz)),
                dma((rounds, nz)), dma((rounds, nz)),
                dma((rounds, nz)), dma((rounds, nz)),
                dma((nu, nz)), dma((nu, nz)),
                dma((nu, nz)), dma((nu, nz)),
            ],
            compiler_params=pltpu.CompilerParams(collective_id=0, has_side_effects=True),
        )(inv, item_factors, item_gram, tile_values.reshape(slots, side, side))
        return sol, item[None]

    return local


def solution(mesh):
    return jax.shard_map(
        make_local(mesh.shape["user"], mesh.shape["item"]),
        mesh=mesh,
        in_specs=(
            P("item", None),
            P(),
            P("user", "item", None),
            P("user", "item", None),
            P("user", "item"),
            P("user", "item", None, None, None),
        ),
        out_specs=(P(("user", "item"), None), P("item", "user", None)),
        check_vma=False,
    )
```

time: 331 us -> 78.3 us (0.24); the launches traced: 325 us -> 78.1 us
  waiting for transfers between devices: 157 us -> 0 us
  Pallas kernels: 0 us -> 72.1 us
  matrix products: 70.4 us -> 0 us
  blocking collectives: 57.9 us -> 0 us
  local copies, waits for them, and re-layouts: 18.7 us -> 3.34 us
  between operations: 14.9 us -> 1.29 us
  other arithmetic: 6.15 us -> 1.29 us
    reduce_scatter x5 -> x0, waiting for transfers between devices: 157 us -> none  [the longest x4 123 us: reduce_rows(): lax.psum_scatter(partial_value, 'item', scatter_dimension=0, tiled=True)]
    pallas_call x0 -> x1, Pallas kernels: none -> 72.1 us  [local(): pl.pallas_call(functools.partial(kernel, nu, ni, scale), out_shape=(jax.S...]
    dot_general x13 -> x0, matrix products: 70.4 us -> none  [the longest x3 25.1 us: apply_work(): jnp.einsum('tui,tir->tur', weighted, item_rows, preferred_element_type=jn...]
    all_gather x4 -> x0, blocking collectives: 57.9 us -> none  [spread_rows(): return lax.all_gather(user_rows, 'item', axis=0, tiled=True)]
    gather x5 -> x0, local copies, waits for them, and re-layouts: 12.5 us -> none  [the longest x3 7.44 us: apply_work(): user_rows = jnp.take(dir_rows, users_here, axis=0)]
    dot_general x5 -> x0, local copies, waits for them, and re-layouts: 6.12 us -> none  [the longest x3 2.66 us: apply_work(): jnp.einsum('tk,tur->kur', chosen_of(users_here, active, USER_BLK), return...]
    unnamed x12 -> x2, local copies, waits for them, and re-layouts: 0.03 us -> 3.34 us
  transfers between devices with their start and end apart: 5 -> 0, of which waited for: 5 -> 0; matrix products, arithmetic and copies ran while one was open for 0% -> 0% of each run, Pallas kernels for 0% -> 0%
where the time goes in v1:
time: 78.3 us; the launch traced here: 78.1 us
  Pallas kernels  72.1 us (92%)
  local copies, waits for them, and re-layouts  3.34 us (4%)
  other arithmetic  1.29 us (2%)
  between operations  1.29 us (2%)
    pallas_call x1, Pallas kernels, local(): pl.pallas_call(functools.partial(kernel, nu, ni, scale), out_shape=(jax.S...  72.1 us
    unnamed x2, local copies, waits for them, and re-layouts  3.34 us

profile of v1, /device:TPU:0, one launch (start us, length us, event | category | flops | bytes accessed | tf_op | source)
XLA Modules:
  0.0 78.1 jit_solution(11910182442725302513)
XLA Ops:
  1.3 0.7 compare_select_fusion
  2.0 0.1 select_reduce_fusion
  2.1 0.5 broadcast_subtract_fusion.inv_ref
  2.6 72.1 %shard_map.77 = (f32[64,256]{1,0:T(8,128)}, f32[512,256]{1,0:T(8,128)}) custom-call(s32[64]{0:T(128)} %broadcast_subtract_fusion.inv_ref, bf16[2048,256]{1,0:T(8,128)(2,1)} %y_hbm.1, f32[256,256]{1,0:T(8,128)} %gram_hbm.1, bf16[48,128,128]{2,1,0:T(8,128)(2,1)} %bitcast.6), custom_call_target="tpu_custom_call" | custom-call | tf_op jit(solution)/shard_map/pallas_call | solution.py:281
  74.7 1.5 %copy.11 = f32[64,256]{1,0:T(8,128)} copy(f32[64,256]{1,0:T(8,128)} %get-tuple-element.10) | data formatting | bytes 131072
  76.2 1.9 %copy.12 = f32[1,512,256]{2,1,0:T(8,128)} copy(f32[1,512,256]{2,1,0:T(8,128)} %bitcast.7) | data formatting | bytes 1048576

commit v2 on v1

v2 whole, which is shorter than its diff:
```python
import functools

import jax
import jax.numpy as jnp
from jax import lax
from jax.experimental import pallas as pl
from jax.experimental.pallas import tpu as pltpu
from jax.sharding import PartitionSpec as P

USER_BLK = 4
ITERS = 3
CHUNK = 256
STREAMS = 2

epsilon = 1e-06
highest = lax.Precision.HIGHEST
MESH = pl.DeviceIdType.MESH
NT = (((1,), (1,)), ((), ()))


def confidence_of(w):
    w = w.astype(jnp.float32)
    return jnp.where(w > 0, 1.0 + w, 0.0).astype(jnp.bfloat16)


def kernel(
    nu, ni, scale,
    inv_ref, y_hbm, gram_hbm, tiles_hbm,
    sol_ref, item_ref,
    tiles, yv, gram, wide, wx, ct, xall, dirs, part, ra, sb, rb,
    d_state, r_state, x_state, n_state, i_state, sol_in,
    load_sem, w_send, w_recv, a_send, a_recv, b_send, b_recv,
    z_send, z_recv, f_send, f_recv, u_send, u_recv, s_send, s_recv, o_send, o_recv,
):
    slots, side, _ = tiles_hbm.shape
    items, rank = yv.shape
    group = wide.shape[0]
    rows = group // ni
    nz = ni // 2
    owners = nz // STREAMS
    low = (nz - owners) // 2
    stream_rows = group // STREAMS
    cols = items // nu
    blocks = items // side
    g, o = lax.axis_index("user"), lax.axis_index("item")
    z, c = lax.div(o, 2), lax.rem(o, 2)
    other = 1 - c
    sib = {"item": z * 2 + other}
    place = lax.rem(z - low + nz, owners)
    is_owner = (z >= low) & (z < low + owners)

    def znum(j):
        return lax.rem(z + (j + nz), nz)

    def unum(j):
        return lax.rem(g + (j + nu), nu)

    def zpeer(j):
        return {"item": znum(j) * 2 + c}

    def upeer(j):
        return {"user": unum(j)}

    def at_row(s, cc, q, base=0):
        return pl.ds(pl.multiple_of(base + ((s * 2 + cc) * owners + q) * rows, rows), rows)

    def half_rows(s, cc):
        size = owners * rows
        return pl.ds(pl.multiple_of((s * 2 + cc) * size, size), size)

    sent = []

    def rcopy(src, dst, ss, rs, dev):
        return pltpu.make_async_remote_copy(
            src_ref=src, dst_ref=dst, send_sem=ss, recv_sem=rs, device_id=dev, device_id_type=MESH
        )

    def send(*args):
        cp = rcopy(*args)
        cp.start()
        sent.append((None, cp))

    def send_if(cond, *args):
        cp = rcopy(*args)
        pl.when(cond)(cp.start)
        sent.append((cond, cp))

    def arrived(dst, ss, rs, dev):
        rcopy(dst, dst, ss, rs, dev).wait_recv()

    loads = [
        pltpu.make_async_copy(tiles_hbm, tiles.at[pl.ds(0, slots)], load_sem.at[0]),
        pltpu.make_async_copy(y_hbm, yv, load_sem.at[1]),
        pltpu.make_async_copy(gram_hbm, gram, load_sem.at[2]),
    ]
    for cp in loads:
        cp.start()

    barrier = pltpu.get_barrier_semaphore()
    pl.semaphore_signal(barrier, inc=1, device_id=sib, device_id_type=MESH)
    for j in range(1, nz):
        pl.semaphore_signal(barrier, inc=1, device_id=zpeer(j), device_id_type=MESH)
    for j in range(1, nu):
        pl.semaphore_signal(barrier, inc=1, device_id=upeer(j), device_id_type=MESH)

    tiles[slots] = jnp.zeros((side, side), jnp.bfloat16)
    loads[0].wait()
    for b in range(blocks):
        for q in range(owners):
            for s in range(STREAMS):
                for cc in range(2):
                    start = ((q * STREAMS + s) * 2 + cc) * rows
                    to = ((s * 2 + cc) * owners + q) * rows
                    u, off = start // side, start % side
                    wide[to : to + rows, b * side : (b + 1) * side] = tiles[
                        inv_ref[u * blocks + b], off : off + rows, :
                    ]
    for cp in loads[1:]:
        cp.wait()

    def wcol(gg):
        return pl.ds(pl.multiple_of(gg * cols, cols), cols)

    def turn(j):
        if j == 0:
            block = wide[:, wcol(g)]
        else:
            arrived(wx.at[j], w_send.at[j], w_recv.at[j], upeer(-j))
            block = wx[j]
        ct[j] = confidence_of(block).T

    turns = [[], [], [], []]
    for j in range(nu):
        turns[j * 4 // nu].append(j)

    def step_of(i):
        return pl.ds(pl.multiple_of(i * CHUNK, CHUNK), CHUNK)

    def stream_pass(k, s):
        here = slice(s * stream_rows, (s + 1) * stream_rows)

        def body(i, acc):
            at = step_of(i)
            yc = yv[at, :]
            if k == 0:
                weighted = confidence_of(wide[here, at])
            else:
                scores = lax.dot_general(dirs[k - 1, here], yc, NT, preferred_element_type=jnp.float32)
                weighted = (scores * wide[here, at].astype(jnp.float32)).astype(jnp.bfloat16)
            part[k, here] += jnp.dot(weighted, yc, preferred_element_type=jnp.float32)
            return acc

        part[k, here] = jnp.zeros((stream_rows, rank), jnp.float32)
        lax.fori_loop(0, items // CHUNK, body, 0)
        send(part.at[k, half_rows(s, other)], ra.at[k, s], a_send.at[k, s], a_recv.at[k, s], sib)

    def reduce_start(k, s):
        arrived(ra.at[k, s], a_send.at[k, s], a_recv.at[k, s], sib)
        total = part[k, half_rows(s, c)] + ra[k, s]
        ra[k, s] = total
        sb[k, s] = total.astype(jnp.bfloat16)
        for q in range(owners):
            zo = q + low
            j = lax.rem(zo - z + nz, nz)
            piece = sb.at[k, s, pl.ds(q * rows, rows)]
            send_if(
                z != zo, piece, rb.at[k, s, j], b_send.at[k, s, q], b_recv.at[k, s, j], {"item": zo * 2 + c}
            )

    def reduce_end(k, s):
        own = ra[k, s, pl.ds(pl.multiple_of(place * rows, rows), rows)]
        for j in range(1, nz):
            arrived(rb.at[k, s, j], b_send.at[k, s, 0], b_recv.at[k, s, j], zpeer(-j))
            own = own + rb[k, s, j].astype(jnp.float32)
        return own

    def buffer(k):
        return (xall, g * group) if k == ITERS else (dirs.at[k], 0)

    def gather_start(k, s, value):
        buf, base = buffer(k)
        mine = at_row(s, c, place, base)
        buf[mine, :] = value.astype(jnp.bfloat16)

    def gather_send(k, s):
        buf, base = buffer(k)
        mine = at_row(s, c, place, base)
        for j in range(1, nz):
            send_if(
                is_owner, buf.at[mine], buf.at[mine], z_send.at[k, s, j], z_recv.at[k, s, place], zpeer(j)
            )

    def gather_pass(k, s):
        buf, base = buffer(k)
        for q in range(owners):
            zo = q + low
            piece = at_row(s, c, q, base)

            @pl.when(z != zo)
            def _():
                arrived(buf.at[piece], z_send.at[k, s, 0], z_recv.at[k, s, q], {"item": lax.rem(o + 2, ni)})

            if k == ITERS:
                for v in range(1, nu):
                    send(buf.at[piece], buf.at[piece], u_send.at[v, s, q], u_recv.at[v, s, q], upeer(v))
            send(buf.at[piece], buf.at[piece], f_send.at[k, s, q], f_recv.at[k, s, q], sib)

    def gather_end(k, s):
        buf, base = buffer(k)
        for q in range(owners):
            arrived(buf.at[at_row(s, other, q, base)], f_send.at[k, s, q], f_recv.at[k, s, q], sib)

    def turn_all(which):
        for j in turns[which]:
            turn(j)

    def update(k, s):
        total = reduce_end(k, s)
        if k == 0:
            r_state[s] = total
            d_state[s] = total
            x_state[s] = jnp.zeros_like(total)
            n_state[s] = jnp.sum(total * total, axis=1, keepdims=True)
            gather_start(k, s, total)
            return
        direction = d_state[s]
        image = i_state[s] + total
        norm = n_state[s]
        alpha = norm / (jnp.sum(direction * image, axis=1, keepdims=True) + epsilon)
        sol = x_state[s] + alpha * direction
        x_state[s] = sol
        if k == ITERS:
            gather_start(k, s, sol)
            return
        residual = r_state[s] - alpha * image
        r_state[s] = residual
        norm_next = jnp.sum(residual * residual, axis=1, keepdims=True)
        direction = residual + norm_next / (norm + epsilon) * direction
        d_state[s] = direction
        n_state[s] = norm_next
        gather_start(k, s, direction)

    def grams():
        for s in range(STREAMS):
            i_state[s] = jnp.dot(
                d_state[s], gram[...], precision=highest, preferred_element_type=jnp.float32
            )

    for k in range(ITERS + 1):
        for s in range(STREAMS):
            if k:
                gather_end(k - 1, s)
            elif s == 0:
                pl.semaphore_wait(barrier, nz + nu - 1)
            stream_pass(k, s)
        for s in range(STREAMS):
            reduce_start(k, s)
        if k == 0:
            for j in range(1, nu):
                send(wide.at[:, wcol(unum(j))], wx.at[j], w_send.at[j], w_recv.at[j], upeer(j))
        else:
            pl.when(is_owner)(grams)
        if k == 1:
            turn_all(0)
        elif k == 2:
            turn_all(1)
        elif k == ITERS:
            turn_all(2)
            turn_all(3)
        for s in range(STREAMS):
            pl.when(is_owner)(functools.partial(update, k, s))
            gather_send(k, s)
        for s in range(STREAMS):
            gather_pass(k, s)

    k = ITERS
    for q in range(owners):
        for s in range(STREAMS):
            target = q * STREAMS + s
            if target != q + low:
                send_if(
                    z == q + low, x_state.at[s], sol_in, o_send.at[s], o_recv, {"item": target * 2 + c}
                )

    def finish(v):
        src = unum(-v)
        for s in range(STREAMS):
            for q in range(owners):
                piece = xall.at[at_row(s, other, q, src * group)]
                if v:
                    arrived(piece, s_send.at[v, s, q], s_recv.at[v, s, q], sib)
                else:
                    arrived(piece, f_send.at[k, s, q], f_recv.at[k, s, q], sib)
        here = pl.ds(pl.multiple_of(src * group, group), group)
        return jnp.dot(ct[v], xall[here, :], preferred_element_type=jnp.float32)

    for v in range(1, nu):
        for s in range(STREAMS):
            for q in range(owners):
                piece = xall.at[at_row(s, c, q, unum(-v) * group)]
                arrived(piece, u_send.at[v, s, q], u_recv.at[v, s, q], upeer(-v))
                send(piece, piece, s_send.at[v, s, q], s_recv.at[v, s, q], sib)
        if v == 1:
            item_ref[...] = finish(0)
        else:
            item_ref[...] += finish(v - 1)

    for target in range(nz):
        owner = target // STREAMS + low

        @pl.when(z == target)
        def _():
            if owner == target:
                sol_ref[...] = x_state[target % STREAMS]
            else:
                arrived(sol_in, o_send.at[0], o_recv, {"item": owner * 2 + c})
                sol_ref[...] = sol_in[...]

    item_ref[...] = (item_ref[...] + finish(nu - 1)) * scale
    for cond, cp in sent:
        if cond is None:
            cp.wait_send()
        else:
            pl.when(cond)(cp.wait_send)


def make_local(nu, ni):
    def local(item_factors, item_gram, tile_users, tile_items, tile_counts, tile_values):
        items, rank = item_factors.shape
        slots, side = tile_values.shape[2], tile_values.shape[-1]
        blocks = items // side
        group = USER_BLK * side
        rows = group // ni
        nz = ni // 2
        owners = nz // STREAMS
        cols = items // nu
        at = jnp.arange(slots, dtype=jnp.int32)
        key = jnp.where(at < tile_counts[0, 0], tile_users[0, 0] * blocks + tile_items[0, 0], -1)
        match = key[None, :] == jnp.arange(USER_BLK * blocks, dtype=jnp.int32)[:, None]
        inv = slots - jnp.sum(jnp.where(match, slots - at[None, :], 0), axis=1)
        scale = float(nu * group) ** -0.5
        bf, f4 = jnp.bfloat16, jnp.float32
        dma = pltpu.SemaphoreType.DMA
        rounds = ITERS + 1
        anywhere = pl.BlockSpec(memory_space=pl.ANY)
        vmem = pl.BlockSpec(memory_space=pltpu.VMEM)
        sol, item = pl.pallas_call(
            functools.partial(kernel, nu, ni, scale),
            out_shape=(
                jax.ShapeDtypeStruct((rows, rank), f4),
                jax.ShapeDtypeStruct((cols, rank), f4),
            ),
            in_specs=[pl.BlockSpec(memory_space=pltpu.SMEM), anywhere, anywhere, anywhere],
            out_specs=(vmem, vmem),
            scratch_shapes=[
                pltpu.VMEM((slots + 1, side, side), bf),
                pltpu.VMEM((items, rank), bf),
                pltpu.VMEM((rank, rank), f4),
                pltpu.VMEM((group, items), bf),
                pltpu.VMEM((nu, group, cols), bf),
                pltpu.VMEM((nu, cols, group), bf),
                pltpu.VMEM((nu * group, rank), bf),
                pltpu.VMEM((ITERS, group, rank), bf),
                pltpu.VMEM((rounds, group, rank), f4),
                pltpu.VMEM((rounds, STREAMS, owners * rows, rank), f4),
                pltpu.VMEM((rounds, STREAMS, owners * rows, rank), bf),
                pltpu.VMEM((rounds, STREAMS, nz, rows, rank), bf),
                pltpu.VMEM((STREAMS, rows, rank), f4),
                pltpu.VMEM((STREAMS, rows, rank), f4),
                pltpu.VMEM((STREAMS, rows, rank), f4),
                pltpu.VMEM((STREAMS, rows, 1), f4),
                pltpu.VMEM((STREAMS, rows, rank), f4),
                pltpu.VMEM((rows, rank), f4),
                dma((3,)),
                dma((nu,)), dma((nu,)),
                dma((rounds, STREAMS)), dma((rounds, STREAMS)),
                dma((rounds, STREAMS, owners)), dma((rounds, STREAMS, nz)),
                dma((rounds, STREAMS, nz)), dma((rounds, STREAMS, owners)),
                dma((rounds, STREAMS, owners)), dma((rounds, STREAMS, owners)),
                dma((nu, STREAMS, owners)), dma((nu, STREAMS, owners)),
                dma((nu, STREAMS, owners)), dma((nu, STREAMS, owners)),
                dma((STREAMS,)), dma(()),
            ],
            compiler_params=pltpu.CompilerParams(collective_id=0, has_side_effects=True),
        )(inv, item_factors, item_gram, tile_values.reshape(slots, side, side))
        return sol, item[None]

    return local


def solution(mesh):
    return jax.shard_map(
        make_local(mesh.shape["user"], mesh.shape["item"]),
        mesh=mesh,
        in_specs=(
            P("item", None),
            P(),
            P("user", "item", None),
            P("user", "item", None),
            P("user", "item"),
            P("user", "item", None, None, None),
        ),
        out_specs=(P(("user", "item"), None), P("item", "user", None)),
        check_vma=False,
    )
```

time: 78.3 us -> 80.1 us (1.023)
  Pallas kernels: 72.1 us -> 73.9 us
    pallas_call x1, Pallas kernels: 72.1 us -> 73.9 us  [local(): pl.pallas_call(functools.partial(kernel, nu, ni, scale), out_shape=(jax.S...]
where the time goes in v2:
time: 80.1 us; the launch traced here: 79.8 us
  Pallas kernels  73.9 us (92%)
  local copies, waits for them, and re-layouts  3.34 us (4%)
  other arithmetic  1.29 us (2%)
  between operations  1.29 us (2%)
    pallas_call x1, Pallas kernels, local(): pl.pallas_call(functools.partial(kernel, nu, ni, scale), out_shape=(jax.S...  73.9 us
    unnamed x2, local copies, waits for them, and re-layouts  3.34 us

profile of v2, /device:TPU:0, one launch (start us, length us, event | category | flops | bytes accessed | tf_op | source)
XLA Modules:
  0.0 79.8 jit_solution(4184401625136701089)
XLA Ops:
  1.3 0.7 compare_select_fusion
  2.0 0.1 select_reduce_fusion
  2.1 0.5 broadcast_subtract_fusion.inv_ref
  2.6 73.9 %shard_map.77 = (f32[64,256]{1,0:T(8,128)}, f32[512,256]{1,0:T(8,128)}) custom-call(s32[64]{0:T(128)} %broadcast_subtract_fusion.inv_ref, bf16[2048,256]{1,0:T(8,128)(2,1)} %y_hbm.1, f32[256,256]{1,0:T(8,128)} %gram_hbm.1, bf16[48,128,128]{2,1,0:T(8,128)(2,1)} %bitcast.6), custom_call_target="tpu_custom_call" | custom-call | tf_op jit(solution)/shard_map/pallas_call | solution.py:347
  76.5 1.5 %copy.11 = f32[64,256]{1,0:T(8,128)} copy(f32[64,256]{1,0:T(8,128)} %get-tuple-element.10) | data formatting | bytes 131072
  77.9 1.9 %copy.12 = f32[1,512,256]{2,1,0:T(8,128)} copy(f32[1,512,256]{2,1,0:T(8,128)} %bitcast.7) | data formatting | bytes 1048576

commit v3 on v2

--- a/solution.py
+++ b/solution.py
@@ -9,7 +9,7 @@
 
 USER_BLK = 4
 ITERS = 3
-CHUNK = 256
+CHUNK = 512
 STREAMS = 2
 
 epsilon = 1e-06
@@ -151,8 +151,7 @@
             return acc
 
         part[k, here] = jnp.zeros((stream_rows, rank), jnp.float32)
-        lax.fori_loop(0, items // CHUNK, body, 0)
-        send(part.at[k, half_rows(s, other)], ra.at[k, s], a_send.at[k, s], a_recv.at[k, s], sib)
+        lax.fori_loop(0, items // CHUNK, body, 0, unroll=4)
 
     def reduce_start(k, s):
         arrived(ra.at[k, s], a_send.at[k, s], a_recv.at[k, s], sib)
@@ -250,9 +249,10 @@
         for s in range(STREAMS):
             if k:
                 gather_end(k - 1, s)
-            elif s == 0:
+            stream_pass(k, s)
+            if k == 0 and s == 0:
                 pl.semaphore_wait(barrier, nz + nu - 1)
-            stream_pass(k, s)
+            send(part.at[k, half_rows(s, other)], ra.at[k, s], a_send.at[k, s], a_recv.at[k, s], sib)
         for s in range(STREAMS):
             reduce_start(k, s)
         if k == 0:

time: 80.1 us -> 67 us (0.84)
  Pallas kernels: 73.9 us -> 60.8 us
    pallas_call x1, Pallas kernels: 73.9 us -> 60.8 us  [local(): pl.pallas_call(functools.partial(kernel, nu, ni, scale), out_shape=(jax.S...]
where the time goes in v3:
time: 67 us; the launch traced here: 66.7 us
  Pallas kernels  60.8 us (91%)
  local copies, waits for them, and re-layouts  3.34 us (5%)
  other arithmetic  1.29 us (2%)
  between operations  1.29 us (2%)
    pallas_call x1, Pallas kernels, local(): pl.pallas_call(functools.partial(kernel, nu, ni, scale), out_shape=(jax.S...  60.8 us
    unnamed x2, local copies, waits for them, and re-layouts  3.34 us

profile of v3, /device:TPU:0, one launch (start us, length us, event | category | flops | bytes accessed | tf_op | source)
XLA Modules:
  0.0 66.7 jit_solution(12035436403817115478)
XLA Ops:
  1.3 0.7 %compare_select_fusion = (s32[48]{0:T(128)S(1)}, s32[48]{0:T(128)S(1)}) fusion(s32[1,1,48]{2,1,0:T(1,128)} %param.9, s32[1,1,48]{2,1,0:T(1,128)} %param.8, s32[]{:T(128)} %bitcast.5), kind=kLoop, calls=%fused_computation.2 | loop fusion | flops 240 | bytes 772 | tf_op jit(solution)/shard_map/jit(_where)/select_n | solution.py:338
  2.0 0.1 select_reduce_fusion
  2.1 0.5 broadcast_subtract_fusion.inv_ref
  2.6 60.8 %shard_map.77 = (f32[64,256]{1,0:T(8,128)}, f32[512,256]{1,0:T(8,128)}) custom-call(s32[64]{0:T(128)} %broadcast_subtract_fusion.inv_ref, bf16[2048,256]{1,0:T(8,128)(2,1)} %y_hbm.1, f32[256,256]{1,0:T(8,128)} %gram_hbm.1, bf16[48,128,128]{2,1,0:T(8,128)(2,1)} %bitcast.6), custom_call_target="tpu_custom_call" | custom-call | tf_op jit(solution)/shard_map/pallas_call | solution.py:347
  63.4 1.5 %copy.11 = f32[64,256]{1,0:T(8,128)} copy(f32[64,256]{1,0:T(8,128)} %get-tuple-element.10) | data formatting | bytes 131072
  64.9 1.9 %copy.12 = f32[1,512,256]{2,1,0:T(8,128)} copy(f32[1,512,256]{2,1,0:T(8,128)} %bitcast.7) | data formatting | bytes 1048576

commit v4 on v3

--- a/solution.py
+++ b/solution.py
@@ -322,6 +322,11 @@
             cp.wait_send()
         else:
             pl.when(cond)(cp.wait_send)
+
+
+def place_outputs(sol_in, item_in, sol_out, item_out):
+    sol_out[...] = sol_in[...]
+    item_out[...] = item_in[...]
 
 
 def make_local(nu, ni):
@@ -383,6 +388,15 @@
             ],
             compiler_params=pltpu.CompilerParams(collective_id=0, has_side_effects=True),
         )(inv, item_factors, item_gram, tile_values.reshape(slots, side, side))
+        sol, item = pl.pallas_call(
+            place_outputs,
+            out_shape=(
+                jax.ShapeDtypeStruct((rows, rank), f4),
+                jax.ShapeDtypeStruct((cols, rank), f4),
+            ),
+            in_specs=[vmem, vmem],
+            out_specs=(vmem, vmem),
+        )(sol, item)
         return sol, item[None]
 
     return local

time: 67 us -> 65.5 us (0.978)
  local copies, waits for them, and re-layouts: 3.34 us -> 0 us
  Pallas kernels: 60.8 us -> 62.7 us
    unnamed x2 -> x0, local copies, waits for them, and re-layouts: 3.34 us -> none
    pallas_call x0 -> x1, Pallas kernels: none -> 1.91 us  [local(): pl.pallas_call(place_outputs, out_shape=(jax.ShapeDtypeStruct((rows, rank...]
where the time goes in v4:
time: 65.5 us; the launch traced here: 65.3 us
  Pallas kernels  62.7 us (96%)
  other arithmetic  1.29 us (2%)
  between operations  1.29 us (2%)
    pallas_call x1, Pallas kernels, local(): pl.pallas_call(functools.partial(kernel, nu, ni, scale), out_shape=(jax.S...  60.8 us
    pallas_call x1, Pallas kernels, local(): pl.pallas_call(place_outputs, out_shape=(jax.ShapeDtypeStruct((rows, rank...  1.91 us

profile of v4, /device:TPU:0, one launch (start us, length us, event | category | flops | bytes accessed | tf_op | source)
XLA Modules:
  0.0 65.3 jit_solution(4137677747232133132)
XLA Ops:
  1.3 0.7 %compare_select_fusion = (s32[48]{0:T(128)S(1)}, s32[48]{0:T(128)S(1)}) fusion(s32[1,1,48]{2,1,0:T(1,128)} %param.9, s32[1,1,48]{2,1,0:T(1,128)} %param.8, s32[]{:T(128)} %bitcast.5), kind=kLoop, calls=%fused_computation.2 | loop fusion | flops 240 | bytes 772 | tf_op jit(solution)/shard_map/jit(_where)/select_n | solution.py:343
  2.0 0.1 select_reduce_fusion
  2.1 0.5 broadcast_subtract_fusion.inv_ref
  2.6 60.8 %shard_map.77 = (f32[64,256]{1,0:T(8,128)}, f32[512,256]{1,0:T(8,128)}) custom-call(s32[64]{0:T(128)} %broadcast_subtract_fusion.inv_ref, bf16[2048,256]{1,0:T(8,128)(2,1)} %y_hbm.1, f32[256,256]{1,0:T(8,128)} %gram_hbm.1, bf16[48,128,128]{2,1,0:T(8,128)(2,1)} %bitcast.6), custom_call_target="tpu_custom_call" | custom-call | tf_op jit(solution)/shard_map/pallas_call | solution.py:352
  63.4 1.9 %shard_map.78 = (f32[64,256]{1,0:T(8,128)}, f32[512,256]{1,0:T(8,128)}) custom-call(f32[64,256]{1,0:T(8,128)} %get-tuple-element.6.sol_in, f32[512,256]{1,0:T(8,128)} %get-tuple-element.7.item_in), custom_call_target="tpu_custom_call" | custom-call | tf_op jit(solution)/shard_map/pallas_call | solution.py:391
